TPU v7x, 256 devices: a whole 4x4x8 slice. The times are simulated.
256 devices in a mesh: band: 4 (over y_lo, core), slab: 64 (over z, y_hi, x).
Axes of the slice: x: 4, y: 4 (y_hi: 2, y_lo: 2; y = y_hi * 2 + y_lo), z: 8, core: 2. Of those that a mesh axis runs over, the one named last changes fastest.
Arguments:
- bands: float32 [8, 192, 192, 192], P('band', 'slab'), may hold values from -8 to 8
- occupied: float32 [16, 192, 192, 192], P('band', 'slab'), may hold values from -8 to 8
- occ_index: int32 [2], replicated, may hold values from 0 to 15
- band_pick: int32 [8], P('band'), may hold values from 0 to 1
Outputs:
- exchange_out: float32 [8, 192, 192, 192], P('band', 'slab')
All inputs are finite; a program needn't handle non-finite values.
Results may differ from a plain program's by a relative error of at most 0.0001.
Values sent between devices are 32-bit elements; how exact they have to be, the bound alone decides.
A program may use at most 64 MiB of HBM per device.

v0:
```python
import math
import jax
import jax.numpy as jnp
from jax import lax
from jax.sharding import PartitionSpec as P

grid_step = 0.25
omega = 0.106


def broadcast(x, axis, root):
    mine = lax.axis_index(axis) == root
    return lax.psum(jnp.where(mine, x, jnp.zeros_like(x)), axis)


def wave_squared(length):
    modes = jnp.arange(length, dtype=jnp.int32)
    signed = jnp.where(modes <= length // 2, modes, modes - length)
    wave = 2.0 * math.pi / (length * grid_step) * signed.astype(jnp.float32)
    return wave * wave


def screened(squares):
    nonzero = jnp.where(squares > 0, squares, jnp.ones_like(squares))
    value = 4.0 * math.pi * (1.0 - jnp.exp(-squares / (4.0 * omega * omega))) / nonzero
    return jnp.where(squares > 0, value, jnp.full_like(squares, math.pi / (omega * omega)))


def cas_matrix(length):
    indices = jnp.arange(length, dtype=jnp.int32)
    product = indices[:, None] * indices[None, :] % length
    phases = 2.0 * math.pi / length * product.astype(jnp.float32)
    return jnp.cos(phases) + jnp.sin(phases)


def along_z(values, matrix):
    return jnp.einsum("pxyz,zk->pxyk", values, matrix, precision=lax.Precision.HIGHEST)


def along_y(values, matrix):
    return jnp.einsum("pxyz,yk->pxkz", values, matrix, precision=lax.Precision.HIGHEST)


def along_x(values, matrix):
    return jnp.einsum("pxyz,xk->pkyz", values, matrix, precision=lax.Precision.HIGHEST)


def shards(bands, occupied, occ_index, band_pick):
    points = bands.shape[2]
    planes = bands.shape[1]
    window = occ_index.shape[0]
    per_group = occupied.shape[0]
    matrix = cas_matrix(points)
    squares = wave_squared(points)
    offset = lax.axis_index("slab") * planes
    row_squares = lax.dynamic_slice_in_dim(squares, offset, planes)
    kernel = screened(squares[:, None, None] + row_squares[None, :, None] + squares[None, None, :])
    kernel = kernel / float(points * points * points)
    targets = jnp.take(bands, band_pick, axis=0)

    def fetch_orbital(turn):
        which = occ_index[turn]
        owner_group = which // per_group
        own_orbital = lax.dynamic_index_in_dim(occupied, which % per_group, 0, keepdims=False)
        return broadcast(own_orbital, "band", owner_group)

    def to_spectrum(density):
        return along_y(along_z(density, matrix), matrix)

    def from_spectrum(spectrum):
        return along_z(along_y(spectrum, matrix), matrix)

    def convolve(pencil):
        return along_x(kernel[None] * along_x(pencil, matrix), matrix)

    def back_each(pencil):
        return lax.all_to_all(convolve(pencil), "slab", split_axis=1, concat_axis=2, tiled=True)

    def update(turn, total):
        orbital = fetch_orbital(turn)
        density = targets * orbital[None]
        filtered = back_each(
            lax.all_to_all(to_spectrum(density), "slab", split_axis=2, concat_axis=1, tiled=True)
        )
        return total - from_spectrum(filtered) * orbital[None]

    result = lax.fori_loop(0, window, update, jnp.zeros(targets.shape, jnp.float32))
    return result


def solution(mesh):
    placed = (P("band", "slab", None, None), P("band", "slab", None, None), P(), P("band"))
    return jax.shard_map(
        shards, mesh=mesh, in_specs=placed, out_specs=P("band", "slab", None, None), check_vma=False
    )
```

profile of v0, /device:TPU:6, one launch (start us, length us, event | category | flops | bytes accessed | tf_op | source)
XLA Modules:
  0.0 321.0 jit_solution(7959825404634566891)
XLA Ops:
  6.7 0.7 compare_select_fusion.1
  9.1 305.0 %while.17 = (s32[]{:T(128)}, f32[2,3,192,192]{3,2,1,0:T(8,128)}, s32[2]{0:T(128)S(1)}, f32[4,3,192,192]{3,2,1,0:T(8,128)}, f32[2,3,192,192]{3,2,1,0:T(8,128)S(1)...) while((s32[]{:T(128)}, f32[2,3,192,192]{3,2,1,0:T(8,128)}, ...), condition=%wide.region_2.3_spmd.clone.clone, body=%wide.region_0.2_spmd.clone.clone.sunk | while | flops 3062292480 | bytes 46599840 | solution.py:87
  12.0 1.9 select_bitcast_fusion.2
  14.0 46.4 %all-reduce.2.cloned.1.call-done = f32[3,192,192]{2,1,0:T(8,128)} async-done(((f32[3,192,192]{2,1,0:T(8,128)}), f32[3,192,192]{2,1,0:T(8,128)}) %all-reduce.2.cloned.1.call-update) | async-done | bytes 442384 | tf_op jit(solution)/shard_map/while/body/eval_jaxpr/psum | solution.py:13
  60.4 3.1 fusion.81
  63.5 1.9 convolution_bitcast_fusion.7
  65.4 1.6 copy.44
  67.0 12.7 %all-to-all-start = ((f32[2,3,192,192]{3,0,1,2:T(2,128)}), f32[2,3,192,192]{3,0,1,2:T(2,128)S(1)}, u32[]{:S(2)}, u32[]{:S(2)}) async-start(f32[2,3,192,192]{3,0,1,2:T(2,128)} %copy.44), calls=%async_computation | async-start | bytes 2359296 | tf_op jit(solution)/shard_map/while/body/eval_jaxpr/all_to_all | solution.py:83
  80.0 32.1 %all-to-all-done = f32[2,3,192,192]{3,0,1,2:T(2,128)S(1)} async-done(((f32[2,3,192,192]{3,0,1,2:T(2,128)}), f32[2,3,192,192]{3,0,1,2:T(2,128)S(1)}, u32[]{:S(2)}, u32[]{:S(2)}) %all-to-all-start) | async-done | bytes 884768 | tf_op jit(solution)/shard_map/while/body/eval_jaxpr/all_to_all | solution.py:83
  112.5 3.0 fusion.83
  115.5 1.9 convolution_bitcast_fusion.8
  117.4 1.6 copy.46
  119.0 7.2 %all-to-all-start.1 = ((f32[2,192,3,192]{3,0,2,1:T(2,128)}), f32[2,192,3,192]{3,0,2,1:T(2,128)S(1)}, u32[]{:S(2)}, u32[]{:S(2)}) async-start(f32[2,192,3,192]{3,0,2,1:T(2,128)} %copy.46), calls=%async_computation.1 | async-start | bytes 2359296 | tf_op jit(solution)/shard_map/while/body/eval_jaxpr/all_to_all | solution.py:77
  126.3 31.1 %all-to-all-done.1 = f32[2,192,3,192]{3,0,2,1:T(2,128)S(1)} async-done(((f32[2,192,3,192]{3,0,2,1:T(2,128)}), f32[2,192,3,192]{3,0,2,1:T(2,128)S(1)}, u32[]{:S(2)}, u32[]{:S(2)}) %all-to-all-start.1) | async-done | bytes 884768 | tf_op jit(solution)/shard_map/while/body/eval_jaxpr/all_to_all | solution.py:77
  157.8 3.0 convolution_bitcast_fusion.9
  160.8 3.4 %fusion.84 = f32[2,3,192,192]{3,2,1,0:T(8,128)S(1)} fusion(f32[2,3,192,192]{2,3,1,0:T(8,128)S(1)} %convolution_bitcast_fusion.9, f32[2,3,192,192]{3,2,1,0:T(8,128)S(1)} %copy-done.4, f32[3,192,192]{2,1,0:T(8,128)S(1)} %copy-done.1, pred[]{:T(512)S(6)} %compare.14), kind=kOutput, calls=%fused_computation.4.clone.1 | convolution fusion | flops 510640128 | bytes 3096577 | tf_op jit(solution)/shard_map/while/body/eval_jaxpr/pxyz,zk->pxyk/dot_general | solution.py:37
  164.2 1.0 copy-done.5
  168.1 1.9 select_bitcast_fusion.2
  170.1 39.2 %all-reduce.2.cloned.1.call-done = f32[3,192,192]{2,1,0:T(8,128)} async-done(((f32[3,192,192]{2,1,0:T(8,128)}), f32[3,192,192]{2,1,0:T(8,128)}) %all-reduce.2.cloned.1.call-update) | async-done | bytes 442384 | tf_op jit(solution)/shard_map/while/body/eval_jaxpr/psum | solution.py:13
  209.2 3.1 fusion.81
  212.4 1.9 convolution_bitcast_fusion.7
  214.3 1.6 copy.44
  215.9 12.7 %all-to-all-start = ((f32[2,3,192,192]{3,0,1,2:T(2,128)}), f32[2,3,192,192]{3,0,1,2:T(2,128)S(1)}, u32[]{:S(2)}, u32[]{:S(2)}) async-start(f32[2,3,192,192]{3,0,1,2:T(2,128)} %copy.44), calls=%async_computation | async-start | bytes 2359296 | tf_op jit(solution)/shard_map/while/body/eval_jaxpr/all_to_all | solution.py:83
  228.9 32.1 %all-to-all-done = f32[2,3,192,192]{3,0,1,2:T(2,128)S(1)} async-done(((f32[2,3,192,192]{3,0,1,2:T(2,128)}), f32[2,3,192,192]{3,0,1,2:T(2,128)S(1)}, u32[]{:S(2)}, u32[]{:S(2)}) %all-to-all-start) | async-done | bytes 884768 | tf_op jit(solution)/shard_map/while/body/eval_jaxpr/all_to_all | solution.py:83
  261.3 3.0 fusion.83
  264.4 1.9 convolution_bitcast_fusion.8
  266.3 1.6 copy.46
  267.9 7.2 %all-to-all-start.1 = ((f32[2,192,3,192]{3,0,2,1:T(2,128)}), f32[2,192,3,192]{3,0,2,1:T(2,128)S(1)}, u32[]{:S(2)}, u32[]{:S(2)}) async-start(f32[2,192,3,192]{3,0,2,1:T(2,128)} %copy.46), calls=%async_computation.1 | async-start | bytes 2359296 | tf_op jit(solution)/shard_map/while/body/eval_jaxpr/all_to_all | solution.py:77
  275.1 31.1 %all-to-all-done.1 = f32[2,192,3,192]{3,0,2,1:T(2,128)S(1)} async-done(((f32[2,192,3,192]{3,0,2,1:T(2,128)}), f32[2,192,3,192]{3,0,2,1:T(2,128)S(1)}, u32[]{:S(2)}, u32[]{:S(2)}) %all-to-all-start.1) | async-done | bytes 884768 | tf_op jit(solution)/shard_map/while/body/eval_jaxpr/all_to_all | solution.py:77
  306.6 3.0 convolution_bitcast_fusion.9
  309.7 3.4 %fusion.84 = f32[2,3,192,192]{3,2,1,0:T(8,128)S(1)} fusion(f32[2,3,192,192]{2,3,1,0:T(8,128)S(1)} %convolution_bitcast_fusion.9, f32[2,3,192,192]{3,2,1,0:T(8,128)S(1)} %copy-done.4, f32[3,192,192]{2,1,0:T(8,128)S(1)} %copy-done.1, pred[]{:T(512)S(6)} %compare.14), kind=kOutput, calls=%fused_computation.4.clone.1 | convolution fusion | flops 510640128 | bytes 3096577 | tf_op jit(solution)/shard_map/while/body/eval_jaxpr/pxyz,zk->pxyk/dot_general | solution.py:37
  313.1 1.0 copy-done.5
  (44 shorter events, 5.4 us)
Async XLA Ops:
  6.5 1.3 copy-start
  7.8 0.7 copy-start.6
  8.5 0.7 copy-start.7
  9.1 51.2 %copy-start.2 = (f32[2,3,192,192]{3,2,1,0:T(8,128)}, f32[2,3,192,192]{3,2,1,0:T(8,128)S(1)}, u32[]{:S(2)}) copy-start(f32[2,3,192,192]{3,2,1,0:T(8,128)S(1)} %get-tuple-element.343) | copy-start | bytes 2654212 | tf_op jit(solution)/shard_map/while
  9.1 51.2 %all-reduce.2.cloned.1.call-start = ((), (), s32[]{:S(2)}) async-start(), calls=%async_computation.2 | async-start | bytes 1179648 | tf_op jit(solution)/shard_map/while/body/eval_jaxpr/psum | solution.py:13
  67.0 45.1 %all-to-all-start = ((f32[2,3,192,192]{3,0,1,2:T(2,128)}), f32[2,3,192,192]{3,0,1,2:T(2,128)S(1)}, u32[]{:S(2)}, u32[]{:S(2)}) async-start(f32[2,3,192,192]{3,0,1,2:T(2,128)} %copy.44), calls=%async_computation | async-start | bytes 2359296 | tf_op jit(solution)/shard_map/while/body/eval_jaxpr/all_to_all | solution.py:83
  119.0 38.3 %all-to-all-start.1 = ((f32[2,192,3,192]{3,0,2,1:T(2,128)}), f32[2,192,3,192]{3,0,2,1:T(2,128)S(1)}, u32[]{:S(2)}, u32[]{:S(2)}) async-start(f32[2,192,3,192]{3,0,2,1:T(2,128)} %copy.46), calls=%async_computation.1 | async-start | bytes 2359296 | tf_op jit(solution)/shard_map/while/body/eval_jaxpr/all_to_all | solution.py:77
  157.7 3.1 copy-start.1
  157.8 3.1 copy-start.4
  160.8 4.4 %copy-start.3 = (f32[2,3,192,192]{3,2,1,0:T(8,128)S(1)}, f32[2,3,192,192]{3,2,1,0:T(8,128)}, u32[]{:S(2)}) copy-start(f32[2,3,192,192]{3,2,1,0:T(8,128)} %copy-done.2) | copy-start | bytes 2654212 | tf_op jit(solution)/shard_map/while
  164.2 1.0 copy-start.5
  165.2 44.0 %copy-start.2 = (f32[2,3,192,192]{3,2,1,0:T(8,128)}, f32[2,3,192,192]{3,2,1,0:T(8,128)S(1)}, u32[]{:S(2)}) copy-start(f32[2,3,192,192]{3,2,1,0:T(8,128)S(1)} %get-tuple-element.343) | copy-start | bytes 2654212 | tf_op jit(solution)/shard_map/while
  165.2 44.0 %all-reduce.2.cloned.1.call-start = ((), (), s32[]{:S(2)}) async-start(), calls=%async_computation.2 | async-start | bytes 1179648 | tf_op jit(solution)/shard_map/while/body/eval_jaxpr/psum | solution.py:13
  215.9 45.1 %all-to-all-start = ((f32[2,3,192,192]{3,0,1,2:T(2,128)}), f32[2,3,192,192]{3,0,1,2:T(2,128)S(1)}, u32[]{:S(2)}, u32[]{:S(2)}) async-start(f32[2,3,192,192]{3,0,1,2:T(2,128)} %copy.44), calls=%async_computation | async-start | bytes 2359296 | tf_op jit(solution)/shard_map/while/body/eval_jaxpr/all_to_all | solution.py:83
  267.9 38.3 %all-to-all-start.1 = ((f32[2,192,3,192]{3,0,2,1:T(2,128)}), f32[2,192,3,192]{3,0,2,1:T(2,128)S(1)}, u32[]{:S(2)}, u32[]{:S(2)}) async-start(f32[2,192,3,192]{3,0,2,1:T(2,128)} %copy.46), calls=%async_computation.1 | async-start | bytes 2359296 | tf_op jit(solution)/shard_map/while/body/eval_jaxpr/all_to_all | solution.py:77
  306.6 3.1 copy-start.1
  306.6 3.1 copy-start.4
  309.7 4.4 %copy-start.3 = (f32[2,3,192,192]{3,2,1,0:T(8,128)S(1)}, f32[2,3,192,192]{3,2,1,0:T(8,128)}, u32[]{:S(2)}) copy-start(f32[2,3,192,192]{3,2,1,0:T(8,128)} %copy-done.2) | copy-start | bytes 2654212 | tf_op jit(solution)/shard_map/while
  313.1 1.0 copy-start.5
Sparse Core Ops, SparseCore 0:
  14.1 46.2 all-reduce.1
  170.2 38.9 all-reduce.1
where the time goes:
time: 322 us; the launch traced here: 321 us
  waiting for transfers between devices  212 us (66%)
  starting transfers between devices  39.9 us (12%)
  matrix products  32.8 us (10%)
  between operations  13.4 us (4%)
  local copies, waits for them, and re-layouts  12.8 us (4%)
  other arithmetic  5.52 us (2%)
  loops' own time  4.72 us (1%)
    psum x2, waiting for transfers between devices, broadcast(): return lax.psum(jnp.where(mine, x, jnp.zeros_like(x)), axis)  85.5 us
    all_to_all x2, waiting for transfers between devices, update(): lax.all_to_all(to_spectrum(density), 'slab', split_axis=2, concat_axis=1,...  64.2 us
    all_to_all x2, waiting for transfers between devices, back_each(): lax.all_to_all(convolve(pencil), 'slab', split_axis=1, concat_axis=2, til...  62.1 us
    all_to_all x2, starting transfers between devices, update(): lax.all_to_all(to_spectrum(density), 'slab', split_axis=2, concat_axis=1,...  25.4 us
    all_to_all x2, starting transfers between devices, back_each(): lax.all_to_all(convolve(pencil), 'slab', split_axis=1, concat_axis=2, til...  14.5 us
    dot_general x4, matrix products, along_z(): jnp.einsum('pxyz,zk->pxyk', values, matrix, precision=lax.Precision.HIGHEST)  13 us
    dot_general x4, matrix products, along_x(): jnp.einsum('pxyz,xk->pkyz', values, matrix, precision=lax.Precision.HIGHEST)  9.88 us
    dot_general x4, matrix products, along_y(): jnp.einsum('pxyz,yk->pxkz', values, matrix, precision=lax.Precision.HIGHEST)  9.88 us
  transfers between devices with their start and end apart: 6, of which 6 were waited for; matrix products, arithmetic and copies ran while one was open for 0% of the time, Pallas kernels for 0%

commit v1 on v0

--- a/solution.py
+++ b/solution.py
@@ -80,7 +80,15 @@
         orbital = fetch_orbital(turn)
         density = targets * orbital[None]
         filtered = back_each(
-            lax.all_to_all(to_spectrum(density), "slab", split_axis=2, concat_axis=1, tiled=True)
+            jnp.concatenate(
+                lax.all_to_all(
+                    jnp.stack(jnp.split(to_spectrum(density), lax.axis_size("slab"), axis=2)),
+                    "slab",
+                    0,
+                    0,
+                ),
+                axis=1,
+            )
         )
         return total - from_spectrum(filtered) * orbital[None]
 

time: 322 us -> 323 us (level)
    another operation x0 -> x4, local copies, waits for them, and re-layouts: none -> 3.28 us  [update(): jnp.stack(jnp.split(to_spectrum(density), lax.axis_size('slab'), axis=2))]
where the time goes in v1:
time: 323 us
  waiting for transfers between devices  212 us (66%)
  starting transfers between devices  39.8 us (12%)
  matrix products  32.7 us (10%)
  local copies, waits for them, and re-layouts  13.8 us (4%)
  between operations  13.4 us (4%)
  other arithmetic  5.52 us (2%)
  loops' own time  5.42 us (2%)
    psum x2, waiting for transfers between devices, broadcast(): return lax.psum(jnp.where(mine, x, jnp.zeros_like(x)), axis)  85.5 us
    all_to_all x2, waiting for transfers between devices, update(): lax.all_to_all(jnp.stack(jnp.split(to_spectrum(density), lax.axis_size('s...  64.2 us
    all_to_all x2, waiting for transfers between devices, back_each(): lax.all_to_all(convolve(pencil), 'slab', split_axis=1, concat_axis=2, til...  62.1 us
    all_to_all x2, starting transfers between devices, update(): lax.all_to_all(jnp.stack(jnp.split(to_spectrum(density), lax.axis_size('s...  25.4 us
    all_to_all x2, starting transfers between devices, back_each(): lax.all_to_all(convolve(pencil), 'slab', split_axis=1, concat_axis=2, til...  14.5 us
    dot_general x4, matrix products, along_z(): jnp.einsum('pxyz,zk->pxyk', values, matrix, precision=lax.Precision.HIGHEST)  12.7 us
    dot_general x4, matrix products, along_y(): jnp.einsum('pxyz,yk->pxkz', values, matrix, precision=lax.Precision.HIGHEST)  10.1 us
    dot_general x4, matrix products, along_x(): jnp.einsum('pxyz,xk->pkyz', values, matrix, precision=lax.Precision.HIGHEST)  9.89 us
  transfers between devices with their start and end apart: 6, of which 6 were waited for; matrix products, arithmetic and copies ran while one was open for 0% of the time, Pallas kernels for 0%

profile of v1, /device:TPU:6, one launch (start us, length us, event | category | flops | bytes accessed | tf_op | source)
XLA Modules:
  0.0 322.5 jit_solution(1843550927380560079)
XLA Ops:
  6.7 0.7 compare_select_fusion.1
  9.1 306.6 %while.17 = (s32[]{:T(128)}, f32[2,3,192,192]{3,2,1,0:T(8,128)}, s32[2]{0:T(128)S(1)}, f32[4,3,192,192]{3,2,1,0:T(8,128)}, f32[2,3,192,192]{3,2,1,0:T(8,128)S(1)...) while((s32[]{:T(128)}, f32[2,3,192,192]{3,2,1,0:T(8,128)}, ...), condition=%wide.region_2.3_spmd.clone.clone, body=%wide.region_0.2_spmd.clone.clone.sunk | while | flops 3062292480 | bytes 47965344 | solution.py:95
  12.0 1.9 select_bitcast_fusion.2
  13.9 46.4 %all-reduce.2.cloned.1.call-done = f32[3,192,192]{2,1,0:T(8,128)} async-done(((f32[3,192,192]{2,1,0:T(8,128)}), f32[3,192,192]{2,1,0:T(8,128)}) %all-reduce.2.cloned.1.call-update) | async-done | bytes 442384 | tf_op jit(solution)/shard_map/while/body/eval_jaxpr/psum | solution.py:13
  60.3 3.0 fusion.81
  63.3 2.0 convolution_bitcast_fusion.7
  66.6 1.6 copy.40
  68.2 12.7 %all-to-all-start = ((f32[64,2,3,3,192]{4,1,3,2,0:T(2,128)}), f32[64,2,3,3,192]{4,1,3,2,0:T(2,128)S(1)}, u32[]{:S(2)}, u32[]{:S(2)}) async-start(f32[64,2,3,3,192]{4,1,3,2,0:T(2,128)} %copy.40), calls=%async_computation | async-start | bytes 2359296 | tf_op jit(solution)/shard_map/while/body/eval_jaxpr/all_to_all | solution.py:84
  81.2 32.1 %all-to-all-done = f32[64,2,3,3,192]{4,1,3,2,0:T(2,128)S(1)} async-done(((f32[64,2,3,3,192]{4,1,3,2,0:T(2,128)}), f32[64,2,3,3,192]{4,1,3,2,0:T(2,128)S(1)}, u32[]{:S(2)}, u32[]{:S(2)}) %all-to-all-start) | async-done | bytes 884768 | tf_op jit(solution)/shard_map/while/body/eval_jaxpr/all_to_all | solution.py:84
  113.3 3.0 fusion.83
  116.3 1.9 convolution_bitcast_fusion.8
  118.2 1.6 copy.41
  119.8 7.2 %all-to-all-start.1 = ((f32[2,192,3,192]{3,0,2,1:T(2,128)}), f32[2,192,3,192]{3,0,2,1:T(2,128)S(1)}, u32[]{:S(2)}, u32[]{:S(2)}) async-start(f32[2,192,3,192]{3,0,2,1:T(2,128)} %copy.41), calls=%async_computation.1 | async-start | bytes 2359296 | tf_op jit(solution)/shard_map/while/body/eval_jaxpr/all_to_all | solution.py:77
  127.1 31.1 %all-to-all-done.1 = f32[2,192,3,192]{3,0,2,1:T(2,128)S(1)} async-done(((f32[2,192,3,192]{3,0,2,1:T(2,128)}), f32[2,192,3,192]{3,0,2,1:T(2,128)S(1)}, u32[]{:S(2)}, u32[]{:S(2)}) %all-to-all-start.1) | async-done | bytes 884768 | tf_op jit(solution)/shard_map/while/body/eval_jaxpr/all_to_all | solution.py:77
  158.6 3.0 convolution_bitcast_fusion.9
  161.6 3.4 %fusion.84 = f32[2,3,192,192]{3,2,1,0:T(8,128)S(1)} fusion(f32[2,3,192,192]{2,3,1,0:T(8,128)S(1)} %convolution_bitcast_fusion.9, f32[2,3,192,192]{3,2,1,0:T(8,128)S(1)} %copy-done.4, f32[3,192,192]{2,1,0:T(8,128)S(1)} %copy-done.1, pred[]{:T(512)S(6)} %compare.14), kind=kOutput, calls=%fused_computation.4.clone.1 | convolution fusion | flops 510640128 | bytes 3096577 | tf_op jit(solution)/shard_map/while/body/eval_jaxpr/pxyz,zk->pxyk/dot_general | solution.py:37
  165.0 1.0 copy-done.5
  168.9 1.9 select_bitcast_fusion.2
  170.9 39.1 %all-reduce.2.cloned.1.call-done = f32[3,192,192]{2,1,0:T(8,128)} async-done(((f32[3,192,192]{2,1,0:T(8,128)}), f32[3,192,192]{2,1,0:T(8,128)}) %all-reduce.2.cloned.1.call-update) | async-done | bytes 442384 | tf_op jit(solution)/shard_map/while/body/eval_jaxpr/psum | solution.py:13
  210.0 3.0 fusion.81
  213.0 2.0 convolution_bitcast_fusion.7
  216.2 1.6 copy.40
  217.8 12.7 %all-to-all-start = ((f32[64,2,3,3,192]{4,1,3,2,0:T(2,128)}), f32[64,2,3,3,192]{4,1,3,2,0:T(2,128)S(1)}, u32[]{:S(2)}, u32[]{:S(2)}) async-start(f32[64,2,3,3,192]{4,1,3,2,0:T(2,128)} %copy.40), calls=%async_computation | async-start | bytes 2359296 | tf_op jit(solution)/shard_map/while/body/eval_jaxpr/all_to_all | solution.py:84
  230.8 32.1 %all-to-all-done = f32[64,2,3,3,192]{4,1,3,2,0:T(2,128)S(1)} async-done(((f32[64,2,3,3,192]{4,1,3,2,0:T(2,128)}), f32[64,2,3,3,192]{4,1,3,2,0:T(2,128)S(1)}, u32[]{:S(2)}, u32[]{:S(2)}) %all-to-all-start) | async-done | bytes 884768 | tf_op jit(solution)/shard_map/while/body/eval_jaxpr/all_to_all | solution.py:84
  262.9 3.0 fusion.83
  266.0 1.9 convolution_bitcast_fusion.8
  267.9 1.6 copy.41
  269.5 7.2 %all-to-all-start.1 = ((f32[2,192,3,192]{3,0,2,1:T(2,128)}), f32[2,192,3,192]{3,0,2,1:T(2,128)S(1)}, u32[]{:S(2)}, u32[]{:S(2)}) async-start(f32[2,192,3,192]{3,0,2,1:T(2,128)} %copy.41), calls=%async_computation.1 | async-start | bytes 2359296 | tf_op jit(solution)/shard_map/while/body/eval_jaxpr/all_to_all | solution.py:77
  276.7 31.1 %all-to-all-done.1 = f32[2,192,3,192]{3,0,2,1:T(2,128)S(1)} async-done(((f32[2,192,3,192]{3,0,2,1:T(2,128)}), f32[2,192,3,192]{3,0,2,1:T(2,128)S(1)}, u32[]{:S(2)}, u32[]{:S(2)}) %all-to-all-start.1) | async-done | bytes 884768 | tf_op jit(solution)/shard_map/while/body/eval_jaxpr/all_to_all | solution.py:77
  308.2 3.0 convolution_bitcast_fusion.9
  311.3 3.4 %fusion.84 = f32[2,3,192,192]{3,2,1,0:T(8,128)S(1)} fusion(f32[2,3,192,192]{2,3,1,0:T(8,128)S(1)} %convolution_bitcast_fusion.9, f32[2,3,192,192]{3,2,1,0:T(8,128)S(1)} %copy-done.4, f32[3,192,192]{2,1,0:T(8,128)S(1)} %copy-done.1, pred[]{:T(512)S(6)} %compare.14), kind=kOutput, calls=%fused_computation.4.clone.1 | convolution fusion | flops 510640128 | bytes 3096577 | tf_op jit(solution)/shard_map/while/body/eval_jaxpr/pxyz,zk->pxyk/dot_general | solution.py:37
  314.7 1.0 copy-done.5
  (170 shorter events, 6.3 us)
Async XLA Ops:
  6.5 1.3 copy-start
  6.5 1.9 copy-start.6
  8.5 0.7 copy-start.7
  9.1 54.2 %copy-start.2 = (f32[2,3,192,192]{3,2,1,0:T(8,128)}, f32[2,3,192,192]{3,2,1,0:T(8,128)S(1)}, u32[]{:S(2)}) copy-start(f32[2,3,192,192]{3,2,1,0:T(8,128)S(1)} %get-tuple-element.343) | copy-start | bytes 2654212 | tf_op jit(solution)/shard_map/while
  9.1 51.2 %all-reduce.2.cloned.1.call-start = ((), (), s32[]{:S(2)}) async-start(), calls=%async_computation.2 | async-start | bytes 1179648 | tf_op jit(solution)/shard_map/while/body/eval_jaxpr/psum | solution.py:13
  68.2 45.1 %all-to-all-start = ((f32[64,2,3,3,192]{4,1,3,2,0:T(2,128)}), f32[64,2,3,3,192]{4,1,3,2,0:T(2,128)S(1)}, u32[]{:S(2)}, u32[]{:S(2)}) async-start(f32[64,2,3,3,192]{4,1,3,2,0:T(2,128)} %copy.40), calls=%async_computation | async-start | bytes 2359296 | tf_op jit(solution)/shard_map/while/body/eval_jaxpr/all_to_all | solution.py:84
  119.8 38.3 %all-to-all-start.1 = ((f32[2,192,3,192]{3,0,2,1:T(2,128)}), f32[2,192,3,192]{3,0,2,1:T(2,128)S(1)}, u32[]{:S(2)}, u32[]{:S(2)}) async-start(f32[2,192,3,192]{3,0,2,1:T(2,128)} %copy.41), calls=%async_computation.1 | async-start | bytes 2359296 | tf_op jit(solution)/shard_map/while/body/eval_jaxpr/all_to_all | solution.py:77
  158.5 3.1 copy-start.1
  158.5 3.1 copy-start.4
  161.6 4.4 %copy-start.3 = (f32[2,3,192,192]{3,2,1,0:T(8,128)S(1)}, f32[2,3,192,192]{3,2,1,0:T(8,128)}, u32[]{:S(2)}) copy-start(f32[2,3,192,192]{3,2,1,0:T(8,128)} %copy-done.2) | copy-start | bytes 2654212 | tf_op jit(solution)/shard_map/while
  165.0 1.0 copy-start.5
  166.0 46.9 %copy-start.2 = (f32[2,3,192,192]{3,2,1,0:T(8,128)}, f32[2,3,192,192]{3,2,1,0:T(8,128)S(1)}, u32[]{:S(2)}) copy-start(f32[2,3,192,192]{3,2,1,0:T(8,128)S(1)} %get-tuple-element.343) | copy-start | bytes 2654212 | tf_op jit(solution)/shard_map/while
  166.0 44.0 %all-reduce.2.cloned.1.call-start = ((), (), s32[]{:S(2)}) async-start(), calls=%async_computation.2 | async-start | bytes 1179648 | tf_op jit(solution)/shard_map/while/body/eval_jaxpr/psum | solution.py:13
  217.8 45.1 %all-to-all-start = ((f32[64,2,3,3,192]{4,1,3,2,0:T(2,128)}), f32[64,2,3,3,192]{4,1,3,2,0:T(2,128)S(1)}, u32[]{:S(2)}, u32[]{:S(2)}) async-start(f32[64,2,3,3,192]{4,1,3,2,0:T(2,128)} %copy.40), calls=%async_computation | async-start | bytes 2359296 | tf_op jit(solution)/shard_map/while/body/eval_jaxpr/all_to_all | solution.py:84
  269.5 38.3 %all-to-all-start.1 = ((f32[2,192,3,192]{3,0,2,1:T(2,128)}), f32[2,192,3,192]{3,0,2,1:T(2,128)S(1)}, u32[]{:S(2)}, u32[]{:S(2)}) async-start(f32[2,192,3,192]{3,0,2,1:T(2,128)} %copy.41), calls=%async_computation.1 | async-start | bytes 2359296 | tf_op jit(solution)/shard_map/while/body/eval_jaxpr/all_to_all | solution.py:77
  308.2 3.1 copy-start.1
  308.2 3.1 copy-start.4
  311.3 4.4 %copy-start.3 = (f32[2,3,192,192]{3,2,1,0:T(8,128)S(1)}, f32[2,3,192,192]{3,2,1,0:T(8,128)}, u32[]{:S(2)}) copy-start(f32[2,3,192,192]{3,2,1,0:T(8,128)} %copy-done.2) | copy-start | bytes 2654212 | tf_op jit(solution)/shard_map/while
  314.7 1.0 copy-start.5
Sparse Core Ops, SparseCore 0:
  14.1 46.2 all-reduce.1
  171.0 38.9 all-reduce.1
